TPU v7x, 512 devices: a whole 4x8x8 slice. The times are simulated.
512 devices in a mesh: req: 128 (over y_lo, z, x, core), tp: 4 (over y_hi).
Axes of the slice: x: 4, y: 8 (y_hi: 4, y_lo: 2; y = y_hi * 2 + y_lo), z: 8, core: 2. Of those that a mesh axis runs over, the one named last changes fastest.
Arguments:
- hidden: bfloat16 [128, 128, 2048], P('req', None, 'tp'), may hold values from -600 to 600
- norm_gain: bfloat16 [2048], replicated, may hold values from 0.099609375 to 1.8984375
- w_query: bfloat16 [2048, 2048], P('req', 'tp'), may hold values from -0.125 to 0.125
- w_key: bfloat16 [2048, 512], P('req', 'tp'), may hold values from -0.125 to 0.125
- w_value: bfloat16 [2048, 512], P('req', 'tp'), may hold values from -0.125 to 0.125
- w_out: bfloat16 [2048, 2048], P('tp', 'req'), may hold values from -0.125 to 0.125
- cache_keys: bfloat16 [128, 2048, 512], P('req', None, 'tp'), may hold values from -72 to 72
- cache_values: bfloat16 [128, 2048, 512], P('req', None, 'tp'), may hold values from -6 to 6
- cache_lengths: int32 [128], replicated, may hold values from 1 to 2048, 131072 in all
Outputs:
- attn_out: bfloat16 [128, 128, 2048], P('req', None, 'tp')
- new_keys: bfloat16 [128, 128, 512], P('req', None, 'tp')
- new_values: bfloat16 [128, 128, 512], P('req', None, 'tp')
Inputs may be any that keep to these rules, and one draw needn't show every extreme that they name: `cache_lengths`: one request has exactly 2048 cached positions; all requests together have 128 * 1024.
All inputs are finite; a program needn't handle non-finite values.
Results may differ from a plain program's by a relative error of at most 0.015.
Values may be sent and summed in bfloat16 or wider, within the bound.
A program may use at most 64 MiB of HBM per device.

v0:
```python
import jax
import jax.numpy as jnp
from jax import lax
from jax.sharding import PartitionSpec as P

HD = 64


rope_base = 1000000.0
norm_eps = 1e-05
masked_score = -1e30


def rotate(tensor, cosine_table, sine_table):
    half_width = tensor.shape[-1] // 2
    front_half = tensor[..., :half_width]
    back_half = tensor[..., half_width:]
    return jnp.concatenate(
        [
            front_half * cosine_table - back_half * sine_table,
            back_half * cosine_table + front_half * sine_table,
        ],
        axis=-1,
    )


def phases(length_now, row_count, head_width):
    positions = (length_now + jnp.arange(row_count, dtype=jnp.int32)).astype(jnp.float32)
    inverse = rope_base ** (
        -jnp.arange(0, head_width, 2, dtype=jnp.int32).astype(jnp.float32) / head_width
    )
    phase_grid = positions[:, None] * inverse[None, :]
    return (jnp.cos(phase_grid)[:, None, :], jnp.sin(phase_grid)[:, None, :])


def group_queries(flat_queries, key_heads, group_size, head_width):
    token_count = flat_queries.shape[0]
    shaped = flat_queries.reshape(token_count, key_heads, group_size, head_width).transpose(
        1, 2, 0, 3
    )
    return shaped.reshape(key_heads, group_size * token_count, head_width)


def attend_block(running, grouped, key_block, value_block, visible):
    peak_old, total_old, accum_old = running
    scores = jnp.einsum(
        "gqd,kgd->gqk", grouped, key_block, preferred_element_type=jnp.float32
    ) * grouped.shape[-1] ** (-0.5)
    scores = jnp.where(visible, scores, masked_score)
    peak_new = jnp.maximum(peak_old, jnp.max(scores, axis=-1))
    weights = jnp.where(visible, jnp.exp(scores - peak_new[..., None]), 0.0)
    factor = jnp.exp(peak_old - peak_new)
    total_new = total_old * factor + jnp.sum(weights, axis=-1)
    accum_new = accum_old * factor[:, None, :] + jnp.einsum(
        "gqk,kgd->gdq",
        weights.astype(jnp.bfloat16),
        value_block,
        preferred_element_type=jnp.float32,
    )
    return (peak_new, total_new, accum_new)


def cache_pass(
    running, grouped, key_cache, value_cache, buffer_first, lower_row, upper_row, block_rows
):
    first_block = lower_row // block_rows
    last_block = jnp.where(
        lower_row < upper_row, (upper_row + block_rows - 1) // block_rows, first_block
    )

    def step_body(block_index, running_now):
        position_first = block_index * block_rows
        local_first = position_first - buffer_first
        key_block = lax.dynamic_slice_in_dim(key_cache, local_first, block_rows, 0)
        value_block = lax.dynamic_slice_in_dim(value_cache, local_first, block_rows, 0)
        positions = position_first + jnp.arange(block_rows, dtype=jnp.int32)
        visible = ((positions >= lower_row) & (positions < upper_row))[None, None, :]
        return attend_block(running_now, grouped, key_block, value_block, visible)

    return lax.fori_loop(first_block, last_block, step_body, running)


def new_pass(running, grouped, fresh_keys, fresh_values, token_count, block_rows):
    token_of_row = jnp.arange(grouped.shape[1], dtype=jnp.int32) % token_count
    positions = 0 + jnp.arange(block_rows, dtype=jnp.int32)
    visible = (positions[None, :] <= token_of_row[:, None])[None]
    running = attend_block(running, grouped, fresh_keys, fresh_values, visible)
    return running


def per_device(
    hidden, norm_gain, w_query, w_key, w_value, w_out, cache_keys, cache_values, cache_lengths
):
    token_count = hidden.shape[1]
    gathered = lax.all_gather(hidden[0], "tp", axis=1, tiled=True)
    as_float = gathered.astype(jnp.float32)
    mean_square = jnp.mean(as_float * as_float, axis=-1, keepdims=True)
    normed = (as_float * lax.rsqrt(mean_square + norm_eps) * norm_gain.astype(jnp.float32)).astype(
        jnp.bfloat16
    )
    query_width = w_query.shape[1]
    key_width = w_key.shape[1]
    query_sum = jnp.dot(
        normed,
        lax.all_gather(w_query, "req", axis=0, tiled=True),
        preferred_element_type=jnp.float32,
    )
    key_sum = jnp.dot(
        normed, lax.all_gather(w_key, "req", axis=0, tiled=True), preferred_element_type=jnp.float32
    )
    value_sum = jnp.dot(
        normed,
        lax.all_gather(w_value, "req", axis=0, tiled=True),
        preferred_element_type=jnp.float32,
    )
    device_index = lax.axis_index("req")
    length_own = cache_lengths[device_index]
    head_width = HD
    local_heads = query_width // head_width
    key_heads = key_width // head_width
    group_size = local_heads // key_heads
    cosine_table, sine_table = phases(length_own, token_count, head_width)
    flat_queries = (
        rotate(query_sum.reshape(token_count, local_heads, head_width), cosine_table, sine_table)
        .astype(jnp.bfloat16)
        .reshape(token_count, query_width)
    )
    fresh_keys = rotate(
        key_sum.reshape(token_count, key_heads, head_width), cosine_table, sine_table
    ).astype(jnp.bfloat16)
    fresh_values = value_sum.reshape(token_count, key_heads, head_width).astype(jnp.bfloat16)
    grouped = group_queries(flat_queries, key_heads, group_size, head_width)
    cache_rows = cache_keys.shape[1]
    key_cache = cache_keys[0].reshape(cache_rows, key_heads, head_width)
    value_cache = cache_values[0].reshape(cache_rows, key_heads, head_width)
    block_cache = min(512, cache_rows // 2)
    block_new = min(512, token_count)
    query_count = group_size * token_count
    start_state = (
        jnp.full((key_heads, query_count), masked_score, jnp.float32),
        jnp.zeros((key_heads, query_count), jnp.float32),
        jnp.zeros((key_heads, head_width, query_count), jnp.float32),
    )
    own_part = cache_pass(
        start_state, grouped, key_cache, value_cache, 0, 0, length_own, block_cache
    )
    combined = new_pass(own_part, grouped, fresh_keys, fresh_values, token_count, block_new)
    accumulated = combined[2] / combined[1][:, None, :]
    mixed_heads = (
        accumulated.reshape(key_heads, head_width, group_size, token_count)
        .transpose(3, 0, 2, 1)
        .reshape(token_count, query_width)
        .astype(jnp.bfloat16)
    )
    partial_out = jnp.dot(
        mixed_heads,
        lax.all_gather(w_out, "req", axis=1, tiled=True),
        preferred_element_type=jnp.float32,
    )
    summed = lax.psum_scatter(
        partial_out.astype(jnp.bfloat16), "tp", scatter_dimension=1, tiled=True
    )
    return (
        summed[None],
        fresh_keys.reshape(token_count, key_width)[None],
        fresh_values.reshape(token_count, key_width)[None],
    )


def solution(mesh):
    in_specs = (
        P("req", None, "tp"),
        P(),
        P("req", "tp"),
        P("req", "tp"),
        P("req", "tp"),
        P("tp", "req"),
        P("req", None, "tp"),
        P("req", None, "tp"),
        P(),
    )
    out_specs = (P("req", None, "tp"), P("req", None, "tp"), P("req", None, "tp"))
    return jax.shard_map(
        per_device, mesh=mesh, in_specs=in_specs, out_specs=out_specs, check_vma=False
    )
```

profile of v0, /device:TPU:1, one launch (start us, length us, event | category | flops | bytes accessed | tf_op | source)
XLA Modules:
  0.0 486.6 jit_solution(11970966800645556888)
XLA Ops:
  7.2 0.0 copy-start
  7.2 0.0 copy-start.1
  7.2 0.0 copy-start.2
  7.2 0.0 all-gather.4.cloned.1.call-start
  7.2 0.7 all-gather.4.cloned.1.call-update
  7.9 0.0 all-gather.6.cloned.1.call-start
  8.0 0.7 all-gather.6.cloned.1.call-update
  8.7 0.0 reduce-scatter.2.cloned.1.call-start
  8.7 1.2 dynamic_slice.9
  11.3 0.6 add_convert_fusion.1
  12.0 17.7 %all-gather = bf16[1,128,2048]{2,1,0:T(8,128)(2,1)S(1)} all-gather(bf16[1,128,512]{2,1,0:T(8,128)(2,1)} %param.11), channel_id=2, replica_groups=mesh['req'=128,'tp'=4] {'tp'}, dimensions={2}, use_global_device_ids=true | all-gather | bytes 655360 | tf_op jit(solution)/shard_map/all_gather | solution.py:95
  29.7 0.2 fusion.25
  29.9 0.7 convert_element_type.70
  30.6 1.2 copy.23
  31.8 0.0 copy-done
  31.8 0.2 copy.27
  32.0 0.0 copy-done.1
  32.0 166.8 %all_gather.17 = bf16[2048,128]{1,0:T(8,128)(2,1)S(1)} all-gather(bf16[16,128]{1,0:T(8,128)(2,1)S(1)} %copy-done.1), channel_id=1, replica_groups=mesh['req'=128,'tp'=4] {'req'}, dimensions={0}, use_global_device_ids=true | all-gather | bytes 528384 | tf_op jit(solution)/shard_map/all_gather | solution.py:109
  198.8 0.0 copy-done.2
  198.9 152.5 %all_gather.18 = bf16[2048,128]{1,0:T(8,128)(2,1)S(1)} all-gather(bf16[16,128]{1,0:T(8,128)(2,1)S(1)} %copy-done.2), channel_id=1, replica_groups=mesh['req'=128,'tp'=4] {'req'}, dimensions={0}, use_global_device_ids=true | all-gather | bytes 528384 | tf_op jit(solution)/shard_map/all_gather | solution.py:113
  351.4 0.4 fusion.39
  351.8 0.4 convolution_convert_fusion.1
  352.2 0.1 multiply_cosine_fusion
  352.4 0.0 all-gather.4.cloned.1.call-done
  352.4 2.6 fusion.41
  355.1 0.1 maximum_bitcast_fusion
  355.2 0.1 reshape.148
  355.3 0.3 fusion.43
  355.6 10.4 %while.14 = (s32[]{:T(128)}, f32[2,512]{1,0:T(2,128)S(1)}, f32[2,512]{1,0:T(2,128)S(1)}, f32[2,64,512]{2,1,0:T(8,128)S(1)}, s32[]{:T(128)}, /*index=5*/s32[]{:T(...) while((s32[]{:T(128)}, f32[2,512]{1,0:T(2,128)S(1)}, ...), condition=%wide.region_4.5_spmd, body=%wide.region_1.4_spmd.sunk | while | flops 141168640 | bytes 7277243 | solution.py:80
  355.6 0.7 fusion.60
  356.3 0.5 bitcast_reduce_fusion.2
  356.8 0.6 fusion.61
  357.5 0.7 convolution_add_fusion.3
  358.2 0.7 fusion.60
  358.9 0.5 bitcast_reduce_fusion.2
  359.4 0.6 fusion.61
  360.1 0.7 convolution_add_fusion.3
  360.8 0.7 fusion.60
  361.5 0.5 bitcast_reduce_fusion.2
  362.0 0.6 fusion.61
  362.6 0.7 convolution_add_fusion.3
  363.4 0.7 fusion.60
  364.1 0.5 bitcast_reduce_fusion.2
  364.6 0.6 fusion.61
  365.2 0.7 convolution_add_fusion.3
  366.0 0.1 fusion.28
  366.1 0.3 fusion.24
  366.4 82.2 %all-gather.6.cloned.1.call-done = bf16[512,2048]{0,1:T(8,128)(2,1)} async-done(((bf16[512,16]{0,1:T(8,128)(2,1)}), bf16[512,2048]{0,1:T(8,128)(2,1)}) %all-gather.6.cloned.1.call-update) | async-done | bytes 2097168 | tf_op jit(solution)/shard_map/all_gather | solution.py:157
  448.6 3.2 convolution_convert_fusion
  451.8 0.0 reduce-scatter.2.cloned.1.call-update
  451.8 0.7 copy.30
  452.5 0.7 copy.31
  453.3 26.8 %reduce-scatter.2.cloned.1.call-done = bf16[128,512]{1,0:T(8,128)(2,1)} async-done(((bf16[128,2048]{1,0:T(8,128)(2,1)}), bf16[128,512]{1,0:T(8,128)(2,1)}) %reduce-scatter.2.cloned.1.call-update) | async-done | bytes 131088 | tf_op jit(solution)/shard_map/reduce_scatter | solution.py:160
  (27 shorter events, 0.4 us)
Async XLA Ops:
  7.2 24.6 %copy-start = (bf16[1,2048,128]{2,1,0:T(8,128)(2,1)S(1)}, bf16[1,2048,128]{2,1,0:T(8,128)(2,1)}, u32[]{:S(2)}) copy-start(bf16[1,2048,128]{2,1,0:T(8,128)(2,1)} %param.18) | copy-start | bytes 1572868
  7.2 24.9 %copy-start.1 = (bf16[16,128]{1,0:T(8,128)(2,1)S(1)}, bf16[16,128]{1,0:T(8,128)(2,1)}, u32[]{:S(2)}) copy-start(bf16[16,128]{1,0:T(8,128)(2,1)} %param.14) | copy-start | bytes 12292
  7.2 191.7 %copy-start.2 = (bf16[16,128]{1,0:T(8,128)(2,1)S(1)}, bf16[16,128]{1,0:T(8,128)(2,1)}, u32[]{:S(2)}) copy-start(bf16[16,128]{1,0:T(8,128)(2,1)} %param.15) | copy-start | bytes 12292
  7.2 345.2 %all-gather.4.cloned.1.call-start = ((), (), s32[]{:S(2)}) async-start(), calls=%async_computation.1 | async-start | bytes 2113536 | tf_op jit(solution)/shard_map/all_gather | solution.py:105
  7.9 440.7 %all-gather.6.cloned.1.call-start = ((), (), s32[]{:S(2)}) async-start(), calls=%async_computation.2 | async-start | bytes 2113536 | tf_op jit(solution)/shard_map/all_gather | solution.py:157
  8.7 471.4 %reduce-scatter.2.cloned.1.call-start = ((), (), s32[]{:S(2)}) async-start(), calls=%async_computation.3 | async-start | bytes 655360 | tf_op jit(solution)/shard_map/reduce_scatter | solution.py:160
Sparse Core Ops, SparseCore 0:
  10.2 221.0 all-gather.3
  233.5 215.0 all-gather.5
  452.0 28.0 reduce-scatter.1
where the time goes:
time: 487 us
  blocking collectives  337 us (69%)
  waiting for transfers between devices  110 us (23%)
  between operations  15.3 us (3%)
  matrix products  12.1 us (2%)
  other arithmetic  7.16 us (1%)
    all_gather x1, blocking collectives, per_device(): lax.all_gather(w_key, 'req', axis=0, tiled=True)  167 us
    all_gather x1, blocking collectives, per_device(): lax.all_gather(w_value, 'req', axis=0, tiled=True)  153 us
    all_gather x1, waiting for transfers between devices, per_device(): lax.all_gather(w_out, 'req', axis=1, tiled=True)  82.2 us
    reduce_scatter x1, waiting for transfers between devices, per_device(): lax.psum_scatter(partial_out.astype(jnp.bfloat16), 'tp', scatter_dimensio...  26.8 us
    all_gather x1, blocking collectives, per_device(): gathered = lax.all_gather(hidden[0], 'tp', axis=1, tiled=True)  17.7 us
  transfers between devices with their start and end apart: 3, of which 2 were waited for; matrix products, arithmetic and copies ran while one was open for 4% of the time, Pallas kernels for 0%

commit v1 on v0

v1 whole, which is shorter than its diff:
```python
import functools

import jax
import jax.numpy as jnp
from jax import lax
from jax.experimental import pallas as pl
from jax.experimental.pallas import tpu as pltpu
from jax.sharding import PartitionSpec as P

HD = 64
NY, NZ, NX = 2, 8, 4
N_TP = 4
TOK = 128
ROW_BLOCKS = 4

rope_base = 1000000.0
norm_eps = 1e-05
masked_score = -1e30
MESH = pl.DeviceIdType.MESH


def ring_keys(axis, n):
    keys = []
    for s in range(1, n // 2 + 1):
        for u in (0, 1):
            for d in (1, -1):
                if s < n // 2 or (u == 0) == (d == 1):
                    keys.append((axis, d, s, u))
    return keys


RING = {"x": ring_keys("x", NX), "z": ring_keys("z", NZ)}
SIZE = {"x": NX, "z": NZ}
STAGES = {0: ("x", "z"), 1: ("z", "x")}
PASS = {c: [("own", 0), ("own", 1)] + RING[STAGES[c][1]] for c in (0, 1)}
KEYS = (
    ["local", "core", "y"]
    + RING["x"]
    + RING["z"]
    + [("pass", c) + (k,) for c in (0, 1) for k in PASS[c]]
)
KEY_INDEX = {k: i for i, k in enumerate(KEYS)}


class Place:
    def __init__(self):
        req = lax.axis_index("req")
        self.tp = lax.axis_index("tp")
        self.core = lax.rem(req, 2)
        self.x = lax.rem(lax.div(req, 2), NX)
        self.z = lax.rem(lax.div(req, 2 * NX), NZ)
        self.y = lax.div(req, 2 * NX * NZ)

    def device(self, core=None, x=None, z=None, y=None, tp=None):
        core = self.core if core is None else core
        x = self.x if x is None else x
        z = self.z if z is None else z
        y = self.y if y is None else y
        tp = self.tp if tp is None else tp
        return (((y * NZ + z) * NX + x) * 2 + core, tp)

    def along(self, axis, offset):
        n = SIZE[axis]
        here = self.x if axis == "x" else self.z
        return lax.rem(here + (offset + 2 * n), n)


class Gather:
    def __init__(self, place, loc, buf, send, recv):
        self.place, self.loc, self.buf, self.send, self.recv = place, loc, buf, send, recv

    def first_block(self, c, u, axis, o):
        p = self.place
        yu = p.y if u == 0 else 1 - p.y
        return self.buf.at[c, yu, p.z, o] if axis == "x" else self.buf.at[c, yu, o, p.x]

    def second_block(self, c, u, axis, o):
        p = self.place
        yu = p.y if u == 0 else 1 - p.y
        return self.buf.at[c, yu, o] if axis == "z" else self.buf.at[c, yu, :, o]

    def make(self, c, key):
        p, i = self.place, KEY_INDEX[key]
        if key == "local":
            return pltpu.make_async_copy(
                self.loc.at[c], self.buf.at[c, p.y, p.z, p.x, pl.ds(c * 16, 16)], self.send.at[i]
            )
        if key == "core":
            src = self.loc.at[1 - c]
            dst = self.buf.at[1 - c, p.y, p.z, p.x, pl.ds(c * 16, 16)]
            dev = p.device(core=1 - p.core)
        elif key == "y":
            src = dst = self.buf.at[c, p.y, p.z, p.x]
            dev = p.device(y=1 - p.y)
        elif key[0] == "pass":
            axis = STAGES[c][1]
            if key[2][0] == "own":
                u, o = key[2][1], p.along(axis, 0)
            else:
                _, d, s, u = key[2]
                o = p.along(axis, -d * s)
            src = dst = self.second_block(c, u, axis, o)
            dev = p.device(core=1 - p.core)
        else:
            axis, d, s, u = key
            o = p.along(axis, -d * (s - 1))
            pick = self.first_block if STAGES[c][0] == axis else self.second_block
            src = dst = pick(c, u, axis, o)
            dev = p.device(**{axis: p.along(axis, d)})
        return pltpu.make_async_remote_copy(
            src_ref=src,
            dst_ref=dst,
            send_sem=self.send.at[i],
            recv_sem=self.recv.at[i],
            device_id=dev,
            device_id_type=MESH,
        )

    def start(self, c, key):
        self.make(c, key).start()

    def land(self, c, key):
        self.make(c, key).wait_recv()

    def steps(self, c):
        first, second = STAGES[c]
        out = []

        def begin():
            self.start(c, "core")
            self.start(c, "local")

        def own():
            self.make(c, "local").wait()
            self.land(c, "core")
            for d in (1, -1):
                self.start(c, (first, d, 1, 0))
            self.start(c, "y")

        def other():
            self.land(c, "y")
            for d in (1, -1):
                self.start(c, (first, d, 1, 1))

        def enter_second(u):
            for d in (1, -1):
                self.start(c, (second, d, 1, u))
            self.start(c, ("pass", c, ("own", u)))

        def first_step(s):
            last = s == SIZE[first] // 2
            for key in RING[first]:
                _, d, ks, u = key
                if ks == s:
                    self.land(c, key)
                    if last:
                        enter_second(u)
                    elif (first, d, s + 1, u) in KEY_INDEX:
                        self.start(c, (first, d, s + 1, u))

        def second_step(s):
            for key in RING[second]:
                _, d, ks, u = key
                if ks == s:
                    self.land(c, key)
                    if (second, d, s + 1, u) in KEY_INDEX:
                        self.start(c, (second, d, s + 1, u))
                    self.start(c, ("pass", c, key))

        def finish():
            for k in PASS[1 - c]:
                self.land(1 - c, ("pass", 1 - c, k))
            for k in ["core", "y"] + RING["x"] + RING["z"]:
                self.make(c, k).wait_send()
            for k in PASS[c]:
                self.make(c, ("pass", c, k)).wait_send()

        out += [begin, own, other]
        out += [functools.partial(first_step, s) for s in range(1, SIZE[first] // 2 + 1)]
        out += [functools.partial(second_step, s) for s in range(1, SIZE[second] // 2 + 1)]
        out += [finish]
        return out


N_STEPS = 3 + NX // 2 + NZ // 2 + 1


def rotate(tile, cosine, sine, lane):
    partner = jnp.where((lane % 64) < 32, pltpu.roll(tile, 96, 1), pltpu.roll(tile, 32, 1))
    return tile * cosine + partner * sine


def kernel(
    lengths,
    hidden,
    gain,
    loc_in,
    loc_out,
    cosine,
    sine,
    keys,
    values,
    out,
    new_keys,
    new_values,
    rows,
    buf_in,
    buf_out,
    normed,
    queries,
    mixed_blocks,
    terms,
    landed,
    send_in,
    recv_in,
    send_out,
    recv_out,
    send_tp,
    recv_tp,
):
    place = Place()
    barrier = pltpu.get_barrier_semaphore()
    partners = [place.device(core=1 - place.core), place.device(y=1 - place.y)]
    for axis in ("x", "z"):
        partners += [place.device(**{axis: place.along(axis, d)}) for d in (1, -1)]
    others = [lax.rem(place.tp + d, N_TP) for d in range(N_TP)]
    partners += [place.device(tp=others[d]) for d in range(1, N_TP)]
    for partner in partners:
        pl.semaphore_signal(barrier, inc=1, device_id=partner, device_id_type=MESH)
    pl.semaphore_wait(barrier, len(partners))

    gather_in = Gather(place, loc_in, buf_in, send_in, recv_in)
    gather_out = Gather(place, loc_out, buf_out, send_out, recv_out)
    steps_in = {c: gather_in.steps(c) for c in (0, 1)}
    steps_out = {c: gather_out.steps(c) for c in (0, 1)}

    def run(steps, i):
        for c in (0, 1):
            pl.when(place.core == c)(steps[c][i])

    def hidden_copy(d):
        return pltpu.make_async_remote_copy(
            src_ref=hidden,
            dst_ref=rows.at[place.tp],
            send_sem=send_tp.at[d],
            recv_sem=recv_tp.at[d],
            device_id=place.device(tp=others[d]),
            device_id_type=MESH,
        )

    own_rows = pltpu.make_async_copy(hidden, rows.at[place.tp], send_tp.at[0])

    run(steps_in, 0)
    for d in (2, 1, 3):
        hidden_copy(d).start()
    own_rows.start()
    run(steps_out, 0)
    run(steps_in, 1)
    run(steps_in, 2)
    run(steps_out, 1)
    run(steps_in, 3)
    run(steps_out, 2)
    run(steps_in, 4)

    own_rows.wait()
    for d in (1, 2, 3):
        hidden_copy(d).wait()
    squares = 0.0
    for j in range(N_TP):
        part = rows[j].astype(jnp.float32)
        squares += jnp.sum(part * part, axis=-1, keepdims=True)
    scale = lax.rsqrt(squares * (1.0 / (512 * N_TP)) + norm_eps)
    for j in range(N_TP):
        part = rows[j].astype(jnp.float32)
        normed[j] = (part * scale * gain[:, 512 * j : 512 * (j + 1)].astype(jnp.float32)).astype(
            jnp.bfloat16
        )

    for i in range(5, N_STEPS - 1):
        run(steps_in, i)
    run(steps_out, 3)
    run(steps_in, N_STEPS - 1)

    def project(c):
        total = jnp.zeros((TOK, 384), jnp.float32)
        for j in range(N_TP):
            block = buf_in[c, j // 2, 4 * (j % 2) : 4 * (j % 2) + 4].reshape(512, 384)
            total += jnp.dot(normed[j], block, preferred_element_type=jnp.float32)
        return total

    first, second = project(0), project(1)
    lane = lax.broadcasted_iota(jnp.int32, (TOK, 128), 1)
    low = lane < 64
    cos_table, sin_table = cosine[...], sine[...]
    fresh_keys = rotate(first[:, 256:], cos_table, sin_table, lane).astype(jnp.bfloat16)
    fresh_values = second[:, 256:].astype(jnp.bfloat16)
    new_keys[...] = fresh_keys
    new_values[...] = fresh_values
    for g, half in enumerate((first, second)):
        for pair in range(2):
            tile = rotate(half[:, 128 * pair : 128 * pair + 128], cos_table, sin_table, lane)
            tile = tile.astype(jnp.bfloat16).astype(jnp.float32) * (HD**-0.5)
            swapped = pltpu.roll(tile, 64, 1)
            if g == 0:
                heads = (jnp.where(low, tile, 0.0), jnp.where(low, swapped, 0.0))
            else:
                heads = (jnp.where(low, 0.0, swapped), jnp.where(low, 0.0, tile))
            for k in range(2):
                queries[2 * g + pair, 128 * k : 128 * k + 128, :] = heads[k].astype(jnp.bfloat16)

    length = lengths[lax.axis_index("req")]
    slot = lax.broadcasted_iota(jnp.int32, (1, 2048), 1)
    cache_bias = jnp.where(slot < length, 0.0, masked_score)
    row_token = lax.broadcasted_iota(jnp.int32, (2 * TOK, TOK), 0) % TOK
    new_bias = jnp.where(
        lax.broadcasted_iota(jnp.int32, (2 * TOK, TOK), 1) <= row_token, 0.0, masked_score
    )
    contract_last = (((1,), (1,)), ((), ()))

    def attend(i, carry):
        for k in range(ROW_BLOCKS):

            @pl.when(i == k)
            def _():
                run(steps_out, 4 + k)

        block = queries[i]
        cache_scores = (
            lax.dot_general(block, keys[...], contract_last, preferred_element_type=jnp.float32)
            + cache_bias
        )
        new_scores = (
            lax.dot_general(
                block, new_keys[...], contract_last, preferred_element_type=jnp.float32
            )
            + new_bias
        )
        peak = jnp.maximum(
            jnp.max(cache_scores, axis=-1, keepdims=True),
            jnp.max(new_scores, axis=-1, keepdims=True),
        )
        cache_weights = jnp.exp(cache_scores - peak)
        new_weights = jnp.exp(new_scores - peak)
        total = jnp.sum(cache_weights, axis=-1, keepdims=True) + jnp.sum(
            new_weights, axis=-1, keepdims=True
        )
        mixed = jnp.dot(
            cache_weights.astype(jnp.bfloat16), values[...], preferred_element_type=jnp.float32
        ) + jnp.dot(
            new_weights.astype(jnp.bfloat16), new_values[...], preferred_element_type=jnp.float32
        )
        mixed_blocks[i] = mixed / total
        return carry

    lax.fori_loop(0, ROW_BLOCKS, attend, 0)

    for i in range(8, N_STEPS):
        run(steps_out, i)

    halves = []
    for g in range(2):
        tiles = []
        for pair in range(2):
            even = mixed_blocks[2 * g + pair, :TOK, :]
            odd = mixed_blocks[2 * g + pair, TOK:, :]
            if g == 0:
                tile = jnp.where(low, even, pltpu.roll(odd, 64, 1))
            else:
                tile = jnp.where(low, pltpu.roll(even, 64, 1), odd)
            tiles.append(tile.astype(jnp.bfloat16))
        halves.append(jnp.concatenate(tiles, axis=1))

    def term_copy(d):
        return pltpu.make_async_remote_copy(
            src_ref=terms.at[d - 1],
            dst_ref=landed.at[d - 1],
            send_sem=send_tp.at[3 + d],
            recv_sem=recv_tp.at[3 + d],
            device_id=place.device(tp=others[d]),
            device_id_type=MESH,
        )

    def term(d):
        target = others[d]
        total = jnp.zeros((TOK, 512), jnp.float32)
        for c in range(2):
            block = buf_out[c, lax.div(target, 2), pl.ds(4 * lax.rem(target, 2), 4)]
            total += lax.dot_general(
                halves[c],
                block.reshape(512, 256),
                contract_last,
                preferred_element_type=jnp.float32,
            )
        return total.astype(jnp.bfloat16)

    for d in (2, 1, 3):
        terms[d - 1] = term(d)
        term_copy(d).start()
    summed = term(0).astype(jnp.float32)
    for d in (1, 3, 2):
        term_copy(d).wait()
        summed += landed[d - 1].astype(jnp.float32)
    out[...] = summed.astype(jnp.bfloat16)


def per_device(
    hidden, norm_gain, w_query, w_key, w_value, w_out, cache_keys, cache_values, cache_lengths
):
    length = cache_lengths[lax.axis_index("req")]
    positions = (length + jnp.arange(TOK, dtype=jnp.int32)).astype(jnp.float32)
    inverse = rope_base ** (-jnp.arange(0, HD, 2, dtype=jnp.int32).astype(jnp.float32) / HD)
    phase = positions[:, None] * inverse[None, :]
    cosine, sine = jnp.cos(phase), jnp.sin(phase)
    cosine = jnp.concatenate([cosine] * 4, axis=1)
    sine = jnp.concatenate([-sine, sine] * 2, axis=1)
    loc_in = jnp.stack(
        [
            jnp.concatenate([w_query[:, :256], w_key], axis=1),
            jnp.concatenate([w_query[:, 256:], w_value], axis=1),
        ]
    )
    loc_out = w_out.T.reshape(16, 2, 256).transpose(1, 0, 2)
    vmem = pl.BlockSpec(memory_space=pltpu.VMEM)
    bf16, f32 = jnp.bfloat16, jnp.float32
    n_keys = len(KEYS)
    results = pl.pallas_call(
        kernel,
        out_shape=(
            jax.ShapeDtypeStruct((TOK, 512), bf16),
            jax.ShapeDtypeStruct((TOK, 128), bf16),
            jax.ShapeDtypeStruct((TOK, 128), bf16),
        ),
        in_specs=[pl.BlockSpec(memory_space=pltpu.SMEM)] + [vmem] * 8,
        out_specs=(vmem, vmem, vmem),
        scratch_shapes=[
            pltpu.VMEM((N_TP, TOK, 512), bf16),
            pltpu.VMEM((2, NY, NZ, NX, 32, 384), bf16),
            pltpu.VMEM((2, NY, NZ, NX, 32, 256), bf16),
            pltpu.VMEM((N_TP, TOK, 512), bf16),
            pltpu.VMEM((ROW_BLOCKS, 2 * TOK, 128), bf16),
            pltpu.VMEM((ROW_BLOCKS, 2 * TOK, 128), f32),
            pltpu.VMEM((N_TP - 1, TOK, 512), bf16),
            pltpu.VMEM((N_TP - 1, TOK, 512), bf16),
            pltpu.SemaphoreType.DMA((n_keys,)),
            pltpu.SemaphoreType.DMA((n_keys,)),
            pltpu.SemaphoreType.DMA((n_keys,)),
            pltpu.SemaphoreType.DMA((n_keys,)),
            pltpu.SemaphoreType.DMA((7,)),
            pltpu.SemaphoreType.DMA((7,)),
        ],
        compiler_params=pltpu.CompilerParams(
            collective_id=0, has_side_effects=True, vmem_limit_bytes=56 * 1024 * 1024
        ),
    )(
        cache_lengths,
        hidden[0],
        norm_gain.reshape(1, -1),
        loc_in,
        loc_out,
        cosine,
        sine,
        cache_keys[0],
        cache_values[0],
    )
    return tuple(r[None] for r in results)


def solution(mesh):
    in_specs = (
        P("req", None, "tp"),
        P(),
        P("req", "tp"),
        P("req", "tp"),
        P("req", "tp"),
        P("tp", "req"),
        P("req", None, "tp"),
        P("req", None, "tp"),
        P(),
    )
    out_specs = (P("req", None, "tp"), P("req", None, "tp"), P("req", None, "tp"))
    return jax.shard_map(
        per_device, mesh=mesh, in_specs=in_specs, out_specs=out_specs, check_vma=False
    )
```

time: 487 us -> 98.5 us (0.20)
  blocking collectives: 337 us -> 0 us
  waiting for transfers between devices: 110 us -> 0 us
  Pallas kernels: 0 us -> 88.1 us
  between operations: 15.3 us -> 0.7 us
  matrix products: 12.1 us -> 0 us
    all_gather x3 -> x0, blocking collectives: 337 us -> none  [the longest x1 167 us: per_device(): lax.all_gather(w_key, 'req', axis=0, tiled=True)]
    pallas_call x0 -> x1, Pallas kernels: none -> 88.1 us  [per_device(): pl.pallas_call(kernel, out_shape=(jax.ShapeDtypeStruct((TOK, 512), bf16),...]
    all_gather x2 -> x0, waiting for transfers between devices: 82.2 us -> none  [the longest x1 82.2 us: per_device(): lax.all_gather(w_out, 'req', axis=1, tiled=True)]
    reduce_scatter x1 -> x0, waiting for transfers between devices: 26.8 us -> none  [per_device(): lax.psum_scatter(partial_out.astype(jnp.bfloat16), 'tp', scatter_dimensio...]
    dot_general x14 -> x0, matrix products: 12.1 us -> none  [the longest x1 3.2 us: per_device(): jnp.dot(mixed_heads, lax.all_gather(w_out, 'req', axis=1, tiled=True), pr...]
  transfers between devices with their start and end apart: 3 -> 0, of which waited for: 2 -> 0; matrix products, arithmetic and copies ran while one was open for 4% -> 0% of each run, Pallas kernels for 0% -> 0%
where the time goes in v1:
time: 98.5 us; the launch traced here: 98.1 us
  Pallas kernels  88.1 us (89%)
  local copies, waits for them, and re-layouts  6.88 us (7%)
  other arithmetic  2.39 us (2%)
    pallas_call x1, Pallas kernels, per_device(): pl.pallas_call(kernel, out_shape=(jax.ShapeDtypeStruct((TOK, 512), bf16),...  88.1 us
    unnamed x19, local copies, waits for them, and re-layouts  5.09 us

profile of v1, /device:TPU:1, one launch (start us, length us, event | category | flops | bytes accessed | tf_op | source)
XLA Modules:
  0.0 98.1 jit_solution(2225541203685688283)
XLA Ops:
  0.6 0.0 copy-start.7
  0.6 0.0 copy-start.2
  0.7 0.6 copy-done.7
  1.3 0.6 dynamic_slice.3
  1.9 0.6 add_convert_fusion
  2.5 0.0 copy-start.4
  2.6 0.7 copy-done.4
  3.2 0.6 reshape.25.gain
  3.8 0.0 copy-done.2
  3.8 0.0 copy-start.3
  3.8 0.6 copy.17
  4.4 0.1 copy-done.3
  4.5 0.0 copy-start.5
  4.5 0.0 copy-start.6
  4.6 0.7 copy-done.5
  5.2 0.0 copy-done.6
  5.3 0.6 pad_maximum_fusion.2.loc_in
  5.9 0.3 fusion
  6.2 0.8 pad_maximum_fusion
  7.0 88.1 %shard_map.112 = (bf16[128,512]{1,0:T(8,128)(2,1)}, bf16[128,128]{1,0:T(8,128)(2,1)}, bf16[128,128]{1,0:T(8,128)(2,1)}) custom-call(s32[128]{0:T(128)} %lengths.1, bf16[128,512]{1,0:T(8,128)(2,1)} %bitcast.21, bf16[1,2048]{1,0:T(2,128)(2,1)} %reshape.25.gain, bf16[2,16,384]{2,1,0:T(8,128)(2,1)} %pad_maximum_fusion.2.loc_in, bf16[2,16,256]{2,1,0:T(8,128)(2,1)} %bitcast.23, ...), custom_call_target="tpu_custom_call" | custom-call | tf_op jit(solution)/shard_map/pallas_call | solution.py:426
  95.1 0.0 copy-start.1
  95.2 1.6 %copy.21 = bf16[1,128,512]{2,1,0:T(8,128)(2,1)} copy(bf16[1,128,512]{2,1,0:T(8,128)(2,1)} %bitcast.22) | data formatting | bytes 262144
  96.7 0.0 copy-done.1
  96.7 0.0 copy-start
  96.7 0.6 copy.22
  97.4 0.2 copy-done
  97.5 0.6 copy.23
  (3 shorter events, 0.0 us)
Async XLA Ops:
  0.6 0.7 copy-start.7
  0.6 3.2 %copy-start.2 = (bf16[512,16]{0,1:T(8,128)(2,1)S(1)}, bf16[512,16]{0,1:T(8,128)(2,1)}, u32[]{:S(2)}) copy-start(bf16[512,16]{0,1:T(8,128)(2,1)} %param.14) | copy-start | bytes 49156
  2.5 0.7 copy-start.4
  3.8 0.7 copy-start.3
  4.5 0.7 copy-start.5
  4.5 0.7 copy-start.6
  95.1 1.6 %copy-start.1 = (bf16[128,128]{1,0:T(8,128)(2,1)S(1)}, bf16[128,128]{1,0:T(8,128)(2,1)}, u32[]{:S(2)}) copy-start(bf16[128,128]{1,0:T(8,128)(2,1)} %get-tuple-element.7) | copy-start | bytes 98308
  96.7 0.8 copy-start

commit v2 on v1

--- a/solution.py
+++ b/solution.py
@@ -2,6 +2,7 @@
 
 import jax
 import jax.numpy as jnp
+import numpy as np
 from jax import lax
 from jax.experimental import pallas as pl
 from jax.experimental.pallas import tpu as pltpu
@@ -29,14 +30,24 @@
     return keys
 
 
-RING = {"x": ring_keys("x", NX), "z": ring_keys("z", NZ)}
 SIZE = {"x": NX, "z": NZ}
+RING = {a: ring_keys(a, SIZE[a]) for a in SIZE}
+DIRECT = {
+    a: [
+        ("direct", a, k, u)
+        for u in (0, 1)
+        for k in sorted(range(1, SIZE[a]), key=lambda k: -min(k, SIZE[a] - k))
+    ]
+    for a in SIZE
+}
 STAGES = {0: ("x", "z"), 1: ("z", "x")}
 PASS = {c: [("own", 0), ("own", 1)] + RING[STAGES[c][1]] for c in (0, 1)}
 KEYS = (
-    ["local", "core", "y"]
+    [("local", 0), ("local", 1), ("core", 0), ("core", 1), "y"]
     + RING["x"]
     + RING["z"]
+    + DIRECT["x"]
+    + DIRECT["z"]
     + [("pass", c) + (k,) for c in (0, 1) for k in PASS[c]]
 )
 KEY_INDEX = {k: i for i, k in enumerate(KEYS)}
@@ -66,8 +77,8 @@
 
 
 class Gather:
-    def __init__(self, place, loc, buf, send, recv):
-        self.place, self.loc, self.buf, self.send, self.recv = place, loc, buf, send, recv
+    def __init__(self, place, parts, buf, send, recv):
+        self.place, self.parts, self.buf, self.send, self.recv = place, parts, buf, send, recv
 
     def first_block(self, c, u, axis, o):
         p = self.place
@@ -81,13 +92,15 @@
 
     def make(self, c, key):
         p, i = self.place, KEY_INDEX[key]
-        if key == "local":
-            return pltpu.make_async_copy(
-                self.loc.at[c], self.buf.at[c, p.y, p.z, p.x, pl.ds(c * 16, 16)], self.send.at[i]
-            )
-        if key == "core":
-            src = self.loc.at[1 - c]
-            dst = self.buf.at[1 - c, p.y, p.z, p.x, pl.ds(c * 16, 16)]
+        if key[0] == "local":
+            src, column = self.parts[c][key[1]]
+            columns = pl.ds(column, src.shape[1])
+            dst = self.buf.at[c, p.y, p.z, p.x, pl.ds(c * 16, 16), columns]
+            return pltpu.make_async_copy(src, dst, self.send.at[i])
+        if key[0] == "core":
+            src, column = self.parts[1 - c][key[1]]
+            columns = pl.ds(column, src.shape[1])
+            dst = self.buf.at[1 - c, p.y, p.z, p.x, pl.ds(c * 16, 16), columns]
             dev = p.device(core=1 - p.core)
         elif key == "y":
             src = dst = self.buf.at[c, p.y, p.z, p.x]
@@ -101,11 +114,13 @@
                 o = p.along(axis, -d * s)
             src = dst = self.second_block(c, u, axis, o)
             dev = p.device(core=1 - p.core)
+        elif key[0] == "direct":
+            _, axis, k, u = key
+            src = dst = self.first_block(c, u, axis, p.along(axis, 0))
+            dev = p.device(**{axis: p.along(axis, k)})
         else:
             axis, d, s, u = key
-            o = p.along(axis, -d * (s - 1))
-            pick = self.first_block if STAGES[c][0] == axis else self.second_block
-            src = dst = pick(c, u, axis, o)
+            src = dst = self.second_block(c, u, axis, p.along(axis, -d * (s - 1)))
             dev = p.device(**{axis: p.along(axis, d)})
         return pltpu.make_async_remote_copy(
             src_ref=src,
@@ -124,65 +139,67 @@
 
     def steps(self, c):
         first, second = STAGES[c]
-        out = []
+        n_parts = range(len(self.parts[c]))
 
         def begin():
-            self.start(c, "core")
-            self.start(c, "local")
+            for k in n_parts:
+                self.start(c, ("core", k))
+            for k in n_parts:
+                self.start(c, ("local", k))
 
         def own():
-            self.make(c, "local").wait()
-            self.land(c, "core")
-            for d in (1, -1):
-                self.start(c, (first, d, 1, 0))
+            for k in n_parts:
+                self.make(c, ("local", k)).wait()
+                self.arrive(c, k)
             self.start(c, "y")
+            for key in DIRECT[first]:
+                if key[3] == 0:
+                    self.start(c, key)
 
         def other():
             self.land(c, "y")
-            for d in (1, -1):
-                self.start(c, (first, d, 1, 1))
-
-        def enter_second(u):
-            for d in (1, -1):
-                self.start(c, (second, d, 1, u))
-            self.start(c, ("pass", c, ("own", u)))
-
-        def first_step(s):
-            last = s == SIZE[first] // 2
-            for key in RING[first]:
-                _, d, ks, u = key
-                if ks == s:
-                    self.land(c, key)
-                    if last:
-                        enter_second(u)
-                    elif (first, d, s + 1, u) in KEY_INDEX:
-                        self.start(c, (first, d, s + 1, u))
-
-        def second_step(s):
-            for key in RING[second]:
-                _, d, ks, u = key
-                if ks == s:
-                    self.land(c, key)
-                    if (second, d, s + 1, u) in KEY_INDEX:
-                        self.start(c, (second, d, s + 1, u))
-                    self.start(c, ("pass", c, key))
+            for key in DIRECT[first]:
+                if key[3] == 1:
+                    self.start(c, key)
+
+        def enter_second():
+            for u in (0, 1):
+                for key in DIRECT[first]:
+                    if key[3] == u:
+                        self.land(c, key)
+                for d in (1, -1):
+                    self.start(c, (second, d, 1, u))
+                self.start(c, ("pass", c, ("own", u)))
+
+        def ring_step(keys):
+            for key in keys:
+                _, d, s, u = key
+                self.land(c, key)
+                if (second, d, s + 1, u) in KEY_INDEX:
+                    self.start(c, (second, d, s + 1, u))
+                self.start(c, ("pass", c, key))
 
         def finish():
             for k in PASS[1 - c]:
                 self.land(1 - c, ("pass", 1 - c, k))
-            for k in ["core", "y"] + RING["x"] + RING["z"]:
+            sent = [("core", k) for k in n_parts] + ["y"] + DIRECT[first] + RING[second]
+            for k in sent + [("pass", c, k) for k in PASS[c]]:
                 self.make(c, k).wait_send()
-            for k in PASS[c]:
-                self.make(c, ("pass", c, k)).wait_send()
-
-        out += [begin, own, other]
-        out += [functools.partial(first_step, s) for s in range(1, SIZE[first] // 2 + 1)]
-        out += [functools.partial(second_step, s) for s in range(1, SIZE[second] // 2 + 1)]
-        out += [finish]
-        return out
-
-
-N_STEPS = 3 + NX // 2 + NZ // 2 + 1
+
+        count = RING_STEPS
+        size = -(-len(RING[second]) // count)
+        chunks = [RING[second][i * size : (i + 1) * size] for i in range(count)]
+        return (
+            [begin, own, other, enter_second]
+            + [functools.partial(ring_step, chunk) for chunk in chunks]
+            + [finish]
+        )
+
+    def arrive(self, c, k):
+        self.make(1 - c, ("core", k)).wait_recv()
+
+
+RING_STEPS = 4
 
 
 def rotate(tile, cosine, sine, lane):
@@ -194,16 +211,19 @@
     lengths,
     hidden,
     gain,
-    loc_in,
-    loc_out,
-    cosine,
-    sine,
-    keys,
-    values,
+    inverse,
+    w_query,
+    w_key,
+    w_value,
+    w_out,
+    keys_far,
+    values_far,
     out,
     new_keys,
     new_values,
     rows,
+    keys,
+    values,
     buf_in,
     buf_out,
     normed,
@@ -211,26 +231,49 @@
     mixed_blocks,
     terms,
     landed,
+    cosine,
+    sine,
     send_in,
     recv_in,
     send_out,
     recv_out,
     send_tp,
     recv_tp,
+    cache_sem,
 ):
     place = Place()
+    cache_copies = [
+        pltpu.make_async_copy(keys_far, keys, cache_sem.at[0]),
+        pltpu.make_async_copy(values_far, values, cache_sem.at[1]),
+    ]
     barrier = pltpu.get_barrier_semaphore()
     partners = [place.device(core=1 - place.core), place.device(y=1 - place.y)]
     for axis in ("x", "z"):
-        partners += [place.device(**{axis: place.along(axis, d)}) for d in (1, -1)]
+        partners += [
+            place.device(**{axis: place.along(axis, k)}) for k in range(1, SIZE[axis])
+        ]
     others = [lax.rem(place.tp + d, N_TP) for d in range(N_TP)]
     partners += [place.device(tp=others[d]) for d in range(1, N_TP)]
     for partner in partners:
         pl.semaphore_signal(barrier, inc=1, device_id=partner, device_id_type=MESH)
+    for copy in cache_copies:
+        copy.start()
+
+    lane = lax.broadcasted_iota(jnp.int32, (TOK, 128), 1)
+    position = lengths[lax.axis_index("req")] + lax.broadcasted_iota(jnp.int32, (TOK, 128), 0)
+    phase = position.astype(jnp.float32) * inverse[...]
+    cosine[...] = jnp.cos(phase)
+    sine[...] = jnp.where((lane % 64) < 32, -1.0, 1.0) * jnp.sin(phase)
+
     pl.semaphore_wait(barrier, len(partners))
 
-    gather_in = Gather(place, loc_in, buf_in, send_in, recv_in)
-    gather_out = Gather(place, loc_out, buf_out, send_out, recv_out)
+    parts_in = [
+        [(w_query.at[:, pl.ds(256 * half, 256)], 0), ((w_key, w_value)[half], 256)]
+        for half in (0, 1)
+    ]
+    parts_out = [[(w_out.at[:, pl.ds(256 * half, 256)], 0)] for half in (0, 1)]
+    gather_in = Gather(place, parts_in, buf_in, send_in, recv_in)
+    gather_out = Gather(place, parts_out, buf_out, send_out, recv_out)
     steps_in = {c: gather_in.steps(c) for c in (0, 1)}
     steps_out = {c: gather_out.steps(c) for c in (0, 1)}
 
@@ -251,16 +294,20 @@
     own_rows = pltpu.make_async_copy(hidden, rows.at[place.tp], send_tp.at[0])
 
     run(steps_in, 0)
-    for d in (2, 1, 3):
-        hidden_copy(d).start()
     own_rows.start()
     run(steps_out, 0)
     run(steps_in, 1)
+    run(steps_out, 1)
+    for d in (2, 1, 3):
+        hidden_copy(d).start()
     run(steps_in, 2)
-    run(steps_out, 1)
+    run(steps_out, 2)
     run(steps_in, 3)
-    run(steps_out, 2)
     run(steps_in, 4)
+    run(steps_in, 5)
+    run(steps_out, 3)
+    run(steps_in, 6)
+    run(steps_in, 7)
 
     own_rows.wait()
     for d in (1, 2, 3):
@@ -276,10 +323,8 @@
             jnp.bfloat16
         )
 
-    for i in range(5, N_STEPS - 1):
-        run(steps_in, i)
-    run(steps_out, 3)
-    run(steps_in, N_STEPS - 1)
+    run(steps_in, 8)
+    run(steps_out, 4)
 
     def project(c):
         total = jnp.zeros((TOK, 384), jnp.float32)
@@ -289,7 +334,6 @@
         return total
 
     first, second = project(0), project(1)
-    lane = lax.broadcasted_iota(jnp.int32, (TOK, 128), 1)
     low = lane < 64
     cos_table, sin_table = cosine[...], sine[...]
     fresh_keys = rotate(first[:, 256:], cos_table, sin_table, lane).astype(jnp.bfloat16)
@@ -318,11 +362,11 @@
     contract_last = (((1,), (1,)), ((), ()))
 
     def attend(i, carry):
-        for k in range(ROW_BLOCKS):
+        for k in range(3):
 
             @pl.when(i == k)
             def _():
-                run(steps_out, 4 + k)
+                run(steps_out, 5 + k)
 
         block = queries[i]
         cache_scores = (
@@ -352,10 +396,11 @@
         mixed_blocks[i] = mixed / total
         return carry
 
+    for copy in cache_copies:
+        copy.wait()
     lax.fori_loop(0, ROW_BLOCKS, attend, 0)
 
-    for i in range(8, N_STEPS):
-        run(steps_out, i)
+    run(steps_out, 8)
 
     halves = []
     for g in range(2):
@@ -406,21 +451,10 @@
 def per_device(
     hidden, norm_gain, w_query, w_key, w_value, w_out, cache_keys, cache_values, cache_lengths
 ):
-    length = cache_lengths[lax.axis_index("req")]
-    positions = (length + jnp.arange(TOK, dtype=jnp.int32)).astype(jnp.float32)
-    inverse = rope_base ** (-jnp.arange(0, HD, 2, dtype=jnp.int32).astype(jnp.float32) / HD)
-    phase = positions[:, None] * inverse[None, :]
-    cosine, sine = jnp.cos(phase), jnp.sin(phase)
-    cosine = jnp.concatenate([cosine] * 4, axis=1)
-    sine = jnp.concatenate([-sine, sine] * 2, axis=1)
-    loc_in = jnp.stack(
-        [
-            jnp.concatenate([w_query[:, :256], w_key], axis=1),
-            jnp.concatenate([w_query[:, 256:], w_value], axis=1),
-        ]
-    )
-    loc_out = w_out.T.reshape(16, 2, 256).transpose(1, 0, 2)
+    powers = np.arange(0, HD, 2, dtype=np.float64) / HD
+    inverse = np.tile((rope_base**-powers).astype(np.float32), 4).reshape(1, 128)
     vmem = pl.BlockSpec(memory_space=pltpu.VMEM)
+    far = pl.BlockSpec(memory_space=pl.ANY)
     bf16, f32 = jnp.bfloat16, jnp.float32
     n_keys = len(KEYS)
     results = pl.pallas_call(
@@ -430,10 +464,12 @@
             jax.ShapeDtypeStruct((TOK, 128), bf16),
             jax.ShapeDtypeStruct((TOK, 128), bf16),
         ),
-        in_specs=[pl.BlockSpec(memory_space=pltpu.SMEM)] + [vmem] * 8,
+        in_specs=[pl.BlockSpec(memory_space=pltpu.SMEM), far, vmem, vmem] + [far] * 6,
         out_specs=(vmem, vmem, vmem),
         scratch_shapes=[
             pltpu.VMEM((N_TP, TOK, 512), bf16),
+            pltpu.VMEM((2048, 128), bf16),
+            pltpu.VMEM((2048, 128), bf16),
             pltpu.VMEM((2, NY, NZ, NX, 32, 384), bf16),
             pltpu.VMEM((2, NY, NZ, NX, 32, 256), bf16),
             pltpu.VMEM((N_TP, TOK, 512), bf16),
@@ -441,12 +477,15 @@
             pltpu.VMEM((ROW_BLOCKS, 2 * TOK, 128), f32),
             pltpu.VMEM((N_TP - 1, TOK, 512), bf16),
             pltpu.VMEM((N_TP - 1, TOK, 512), bf16),
+            pltpu.VMEM((TOK, 128), f32),
+            pltpu.VMEM((TOK, 128), f32),
             pltpu.SemaphoreType.DMA((n_keys,)),
             pltpu.SemaphoreType.DMA((n_keys,)),
             pltpu.SemaphoreType.DMA((n_keys,)),
             pltpu.SemaphoreType.DMA((n_keys,)),
             pltpu.SemaphoreType.DMA((7,)),
             pltpu.SemaphoreType.DMA((7,)),
+            pltpu.SemaphoreType.DMA((2,)),
         ],
         compiler_params=pltpu.CompilerParams(
             collective_id=0, has_side_effects=True, vmem_limit_bytes=56 * 1024 * 1024
@@ -455,10 +494,11 @@
         cache_lengths,
         hidden[0],
         norm_gain.reshape(1, -1),
-        loc_in,
-        loc_out,
-        cosine,
-        sine,
+        jnp.asarray(inverse),
+        w_query,
+        w_key,
+        w_value,
+        w_out.T,
         cache_keys[0],
         cache_values[0],
     )

time: 98.5 us -> 77.2 us (0.78)
  Pallas kernels: 88.1 us -> 71.5 us
  local copies, waits for them, and re-layouts: 6.88 us -> 4.25 us
  other arithmetic: 2.39 us -> 0 us
    pallas_call x1, Pallas kernels: 88.1 us -> 71.5 us  [per_device(): pl.pallas_call(kernel, out_shape=(jax.ShapeDtypeStruct((TOK, 512), bf16),...]
    unnamed x19 -> x9, local copies, waits for them, and re-layouts: 5.09 us -> 3.64 us
where the time goes in v2:
time: 77.2 us; the launch traced here: 76.4 us
  Pallas kernels  71.5 us (93%)
  local copies, waits for them, and re-layouts  4.25 us (6%)
    pallas_call x1, Pallas kernels, per_device(): pl.pallas_call(kernel, out_shape=(jax.ShapeDtypeStruct((TOK, 512), bf16),...  71.5 us
    unnamed x9, local copies, waits for them, and re-layouts  3.64 us

profile of v2, /device:TPU:1, one launch (start us, length us, event | category | flops | bytes accessed | tf_op | source)
XLA Modules:
  0.0 76.4 jit_solution(5868409022321856629)
XLA Ops:
  0.6 0.0 copy-start.2
  0.6 0.7 copy-done.2
  1.3 0.6 reshape.9.gain
  1.9 71.5 %shard_map.121 = (bf16[128,512]{1,0:T(8,128)(2,1)}, bf16[128,128]{1,0:T(8,128)(2,1)}, bf16[128,128]{1,0:T(8,128)(2,1)}) custom-call(s32[128]{0:T(128)} %lengths.1, bf16[128,512]{1,0:T(8,128)(2,1)} %bitcast.10, bf16[1,2048]{1,0:T(2,128)(2,1)} %reshape.9.gain, f32[1,128]{1,0:T(1,128)} %constant.2.clone.inverse, bf16[16,512]{1,0:T(8,128)(2,1)} %w_query.1, ...), custom_call_target="tpu_custom_call" | custom-call | tf_op jit(solution)/shard_map/pallas_call | solution.py:460
  73.4 0.0 copy-start.1
  73.4 1.6 %copy.16 = bf16[1,128,512]{2,1,0:T(8,128)(2,1)} copy(bf16[1,128,512]{2,1,0:T(8,128)(2,1)} %bitcast.9) | data formatting | bytes 262144
  75.0 0.0 copy-done.1
  75.0 0.0 copy-start
  75.0 0.6 copy.17
  75.6 0.2 copy-done
  75.8 0.6 copy.18
Async XLA Ops:
  0.6 0.7 copy-start.2
  73.4 1.6 %copy-start.1 = (bf16[128,128]{1,0:T(8,128)(2,1)S(1)}, bf16[128,128]{1,0:T(8,128)(2,1)}, u32[]{:S(2)}) copy-start(bf16[128,128]{1,0:T(8,128)(2,1)} %get-tuple-element.7) | copy-start | bytes 98308
  75.0 0.8 %copy-start = (bf16[128,128]{1,0:T(8,128)(2,1)S(1)}, bf16[128,128]{1,0:T(8,128)(2,1)}, u32[]{:S(2)}) copy-start(bf16[128,128]{1,0:T(8,128)(2,1)} %get-tuple-element.8) | copy-start | bytes 98308

commit v3 on v2

--- a/solution.py
+++ b/solution.py
@@ -13,6 +13,7 @@
 N_TP = 4
 TOK = 128
 ROW_BLOCKS = 4
+HALF = TOK // 2
 
 rope_base = 1000000.0
 norm_eps = 1e-05
@@ -32,22 +33,15 @@
 
 SIZE = {"x": NX, "z": NZ}
 RING = {a: ring_keys(a, SIZE[a]) for a in SIZE}
-DIRECT = {
-    a: [
-        ("direct", a, k, u)
-        for u in (0, 1)
-        for k in sorted(range(1, SIZE[a]), key=lambda k: -min(k, SIZE[a] - k))
-    ]
-    for a in SIZE
-}
+DIRECT = {"x": [("direct", "x", k, u) for u in (0, 1) for k in (2, 1, 3)]}
 STAGES = {0: ("x", "z"), 1: ("z", "x")}
+FIRST = {"x": DIRECT["x"], "z": RING["z"]}
 PASS = {c: [("own", 0), ("own", 1)] + RING[STAGES[c][1]] for c in (0, 1)}
 KEYS = (
     [("local", 0), ("local", 1), ("core", 0), ("core", 1), "y"]
     + RING["x"]
     + RING["z"]
     + DIRECT["x"]
-    + DIRECT["z"]
     + [("pass", c) + (k,) for c in (0, 1) for k in PASS[c]]
 )
 KEY_INDEX = {k: i for i, k in enumerate(KEYS)}
@@ -83,27 +77,27 @@
     def first_block(self, c, u, axis, o):
         p = self.place
         yu = p.y if u == 0 else 1 - p.y
-        return self.buf.at[c, yu, p.z, o] if axis == "x" else self.buf.at[c, yu, o, p.x]
+        return self.buf[c].at[yu, p.z, o] if axis == "x" else self.buf[c].at[yu, o, p.x]
 
     def second_block(self, c, u, axis, o):
         p = self.place
         yu = p.y if u == 0 else 1 - p.y
-        return self.buf.at[c, yu, o] if axis == "z" else self.buf.at[c, yu, :, o]
+        return self.buf[c].at[yu, o] if axis == "z" else self.buf[c].at[yu, :, o]
 
     def make(self, c, key):
         p, i = self.place, KEY_INDEX[key]
         if key[0] == "local":
             src, column = self.parts[c][key[1]]
             columns = pl.ds(column, src.shape[1])
-            dst = self.buf.at[c, p.y, p.z, p.x, pl.ds(c * 16, 16), columns]
+            dst = self.buf[c].at[p.y, p.z, p.x, pl.ds(c * 16, 16), columns]
             return pltpu.make_async_copy(src, dst, self.send.at[i])
         if key[0] == "core":
             src, column = self.parts[1 - c][key[1]]
             columns = pl.ds(column, src.shape[1])
-            dst = self.buf.at[1 - c, p.y, p.z, p.x, pl.ds(c * 16, 16), columns]
+            dst = self.buf[1 - c].at[p.y, p.z, p.x, pl.ds(c * 16, 16), columns]
             dev = p.device(core=1 - p.core)
         elif key == "y":
-            src = dst = self.buf.at[c, p.y, p.z, p.x]
+            src = dst = self.buf[c].at[p.y, p.z, p.x]
             dev = p.device(y=1 - p.y)
         elif key[0] == "pass":
             axis = STAGES[c][1]
@@ -120,7 +114,8 @@
             dev = p.device(**{axis: p.along(axis, k)})
         else:
             axis, d, s, u = key
-            src = dst = self.second_block(c, u, axis, p.along(axis, -d * (s - 1)))
+            pick = self.first_block if axis == STAGES[c][0] else self.second_block
+            src = dst = pick(c, u, axis, p.along(axis, -d * (s - 1)))
             dev = p.device(**{axis: p.along(axis, d)})
         return pltpu.make_async_remote_copy(
             src_ref=src,
@@ -147,29 +142,43 @@
             for k in n_parts:
                 self.start(c, ("local", k))
 
+        def start_first(u):
+            for key in FIRST[first]:
+                if key[3] == u and (key[0] == "direct" or key[2] == 1):
+                    self.start(c, key)
+
         def own():
             for k in n_parts:
                 self.make(c, ("local", k)).wait()
                 self.arrive(c, k)
             self.start(c, "y")
-            for key in DIRECT[first]:
-                if key[3] == 0:
-                    self.start(c, key)
+            start_first(0)
 
         def other():
             self.land(c, "y")
-            for key in DIRECT[first]:
-                if key[3] == 1:
-                    self.start(c, key)
-
-        def enter_second():
+            start_first(1)
+
+        def enter_second(u):
+            for d in (1, -1):
+                self.start(c, (second, d, 1, u))
+            self.start(c, ("pass", c, ("own", u)))
+
+        def after_direct():
             for u in (0, 1):
                 for key in DIRECT[first]:
                     if key[3] == u:
                         self.land(c, key)
-                for d in (1, -1):
-                    self.start(c, (second, d, 1, u))
-                self.start(c, ("pass", c, ("own", u)))
+                enter_second(u)
+
+        def first_step(step):
+            for key in RING[first]:
+                _, d, s, u = key
+                if s == step:
+                    self.land(c, key)
+                    if s == SIZE[first] // 2:
+                        enter_second(u)
+                    elif (first, d, s + 1, u) in KEY_INDEX:
+                        self.start(c, (first, d, s + 1, u))
 
         def ring_step(keys):
             for key in keys:
@@ -182,24 +191,21 @@
         def finish():
             for k in PASS[1 - c]:
                 self.land(1 - c, ("pass", 1 - c, k))
-            sent = [("core", k) for k in n_parts] + ["y"] + DIRECT[first] + RING[second]
+            sent = [("core", k) for k in n_parts] + ["y"] + FIRST[first] + RING[second]
             for k in sent + [("pass", c, k) for k in PASS[c]]:
                 self.make(c, k).wait_send()
 
-        count = RING_STEPS
-        size = -(-len(RING[second]) // count)
-        chunks = [RING[second][i * size : (i + 1) * size] for i in range(count)]
-        return (
-            [begin, own, other, enter_second]
-            + [functools.partial(ring_step, chunk) for chunk in chunks]
-            + [finish]
-        )
+        if first == "x":
+            middle = [after_direct]
+        else:
+            middle = [functools.partial(first_step, i) for i in range(1, SIZE[first] // 2 + 1)]
+        for i in range(1, SIZE[second] // 2 + 1):
+            middle.append(functools.partial(ring_step, [k for k in RING[second] if k[2] == i]))
+        middle += [lambda: None] * (6 - len(middle))
+        return [begin, own, other] + middle + [finish]
 
     def arrive(self, c, k):
         self.make(1 - c, ("core", k)).wait_recv()
-
-
-RING_STEPS = 4
 
 
 def rotate(tile, cosine, sine, lane):
@@ -224,8 +230,10 @@
     rows,
     keys,
     values,
-    buf_in,
-    buf_out,
+    buf_in_0,
+    buf_in_1,
+    buf_out_0,
+    buf_out_1,
     normed,
     queries,
     mixed_blocks,
@@ -250,7 +258,9 @@
     partners = [place.device(core=1 - place.core), place.device(y=1 - place.y)]
     for axis in ("x", "z"):
         partners += [
-            place.device(**{axis: place.along(axis, k)}) for k in range(1, SIZE[axis])
+            place.device(**{axis: place.along(axis, k)})
+            for k in range(1, SIZE[axis])
+            if axis == "x" or k in (1, SIZE[axis] - 1)
         ]
     others = [lax.rem(place.tp + d, N_TP) for d in range(N_TP)]
     partners += [place.device(tp=others[d]) for d in range(1, N_TP)]
@@ -271,7 +281,8 @@
         [(w_query.at[:, pl.ds(256 * half, 256)], 0), ((w_key, w_value)[half], 256)]
         for half in (0, 1)
     ]
-    parts_out = [[(w_out.at[:, pl.ds(256 * half, 256)], 0)] for half in (0, 1)]
+    parts_out = [[(w_out.at[:, pl.ds(0, 128)], 0)], [(w_out.at[:, pl.ds(128, 384)], 0)]]
+    buf_in, buf_out = (buf_in_0, buf_in_1), (buf_out_0, buf_out_1)
     gather_in = Gather(place, parts_in, buf_in, send_in, recv_in)
     gather_out = Gather(place, parts_out, buf_out, send_out, recv_out)
     steps_in = {c: gather_in.steps(c) for c in (0, 1)}
@@ -297,17 +308,22 @@
     own_rows.start()
     run(steps_out, 0)
     run(steps_in, 1)
+    run(steps_in, 2)
     run(steps_out, 1)
     for d in (2, 1, 3):
         hidden_copy(d).start()
-    run(steps_in, 2)
+    run(steps_in, 3)
     run(steps_out, 2)
-    run(steps_in, 3)
     run(steps_in, 4)
+    run(steps_out, 3)
     run(steps_in, 5)
-    run(steps_out, 3)
+    run(steps_out, 4)
     run(steps_in, 6)
+    run(steps_out, 5)
     run(steps_in, 7)
+    run(steps_out, 6)
+    run(steps_in, 8)
+    run(steps_out, 7)
 
     own_rows.wait()
     for d in (1, 2, 3):
@@ -323,13 +339,12 @@
             jnp.bfloat16
         )
 
-    run(steps_in, 8)
-    run(steps_out, 4)
+    run(steps_in, 9)
 
     def project(c):
         total = jnp.zeros((TOK, 384), jnp.float32)
         for j in range(N_TP):
-            block = buf_in[c, j // 2, 4 * (j % 2) : 4 * (j % 2) + 4].reshape(512, 384)
+            block = buf_in[c][j // 2, 4 * (j % 2) : 4 * (j % 2) + 4].reshape(512, 384)
             total += jnp.dot(normed[j], block, preferred_element_type=jnp.float32)
         return total
 
@@ -350,24 +365,20 @@
             else:
                 heads = (jnp.where(low, 0.0, swapped), jnp.where(low, 0.0, tile))
             for k in range(2):
-                queries[2 * g + pair, 128 * k : 128 * k + 128, :] = heads[k].astype(jnp.bfloat16)
+                head = heads[k].astype(jnp.bfloat16)
+                row = HALF * (2 * pair + k)
+                for t in range(2):
+                    queries[2 * t + g, row : row + HALF, :] = head[HALF * t : HALF * (t + 1)]
 
     length = lengths[lax.axis_index("req")]
     slot = lax.broadcasted_iota(jnp.int32, (1, 2048), 1)
     cache_bias = jnp.where(slot < length, 0.0, masked_score)
-    row_token = lax.broadcasted_iota(jnp.int32, (2 * TOK, TOK), 0) % TOK
-    new_bias = jnp.where(
-        lax.broadcasted_iota(jnp.int32, (2 * TOK, TOK), 1) <= row_token, 0.0, masked_score
-    )
+    row_token = lax.broadcasted_iota(jnp.int32, (2 * TOK, TOK), 0) % HALF
+    new_slot = lax.broadcasted_iota(jnp.int32, (2 * TOK, TOK), 1)
     contract_last = (((1,), (1,)), ((), ()))
 
     def attend(i, carry):
-        for k in range(3):
-
-            @pl.when(i == k)
-            def _():
-                run(steps_out, 5 + k)
-
+        pl.when(i == 0)(lambda: run(steps_out, 8))
         block = queries[i]
         cache_scores = (
             lax.dot_general(block, keys[...], contract_last, preferred_element_type=jnp.float32)
@@ -377,7 +388,7 @@
             lax.dot_general(
                 block, new_keys[...], contract_last, preferred_element_type=jnp.float32
             )
-            + new_bias
+            + jnp.where(new_slot <= row_token + HALF * lax.div(i, 2), 0.0, masked_score)
         )
         peak = jnp.maximum(
             jnp.max(cache_scores, axis=-1, keepdims=True),
@@ -398,54 +409,61 @@
 
     for copy in cache_copies:
         copy.wait()
-    lax.fori_loop(0, ROW_BLOCKS, attend, 0)
-
-    run(steps_out, 8)
-
-    halves = []
-    for g in range(2):
+    low = lax.broadcasted_iota(jnp.int32, (HALF, 128), 1) < 64
+
+    def mixed_rows(t):
         tiles = []
-        for pair in range(2):
-            even = mixed_blocks[2 * g + pair, :TOK, :]
-            odd = mixed_blocks[2 * g + pair, TOK:, :]
-            if g == 0:
-                tile = jnp.where(low, even, pltpu.roll(odd, 64, 1))
-            else:
-                tile = jnp.where(low, pltpu.roll(even, 64, 1), odd)
-            tiles.append(tile.astype(jnp.bfloat16))
-        halves.append(jnp.concatenate(tiles, axis=1))
-
-    def term_copy(d):
+        for g in range(2):
+            for pair in range(2):
+                row = 2 * HALF * pair
+                even = mixed_blocks[2 * t + g, row : row + HALF, :]
+                odd = mixed_blocks[2 * t + g, row + HALF : row + 2 * HALF, :]
+                if g == 0:
+                    tile = jnp.where(low, even, pltpu.roll(odd, 64, 1))
+                else:
+                    tile = jnp.where(low, pltpu.roll(even, 64, 1), odd)
+                tiles.append(tile.astype(jnp.bfloat16))
+        return tiles[0], jnp.concatenate(tiles[1:], axis=1)
+
+    def term_copy(t, d):
         return pltpu.make_async_remote_copy(
-            src_ref=terms.at[d - 1],
-            dst_ref=landed.at[d - 1],
-            send_sem=send_tp.at[3 + d],
-            recv_sem=recv_tp.at[3 + d],
+            src_ref=terms.at[d - 1, pl.ds(HALF * t, HALF)],
+            dst_ref=landed.at[d - 1, pl.ds(HALF * t, HALF)],
+            send_sem=send_tp.at[1 + 3 * (t + 1) + d - 1],
+            recv_sem=recv_tp.at[1 + 3 * (t + 1) + d - 1],
             device_id=place.device(tp=others[d]),
             device_id_type=MESH,
         )
 
-    def term(d):
+    def term(shares, d):
         target = others[d]
-        total = jnp.zeros((TOK, 512), jnp.float32)
+        total = jnp.zeros((HALF, 512), jnp.float32)
         for c in range(2):
-            block = buf_out[c, lax.div(target, 2), pl.ds(4 * lax.rem(target, 2), 4)]
+            block = buf_out[c][lax.div(target, 2), pl.ds(4 * lax.rem(target, 2), 4)]
             total += lax.dot_general(
-                halves[c],
-                block.reshape(512, 256),
+                shares[c],
+                block.reshape(512, block.shape[-1]),
                 contract_last,
                 preferred_element_type=jnp.float32,
             )
         return total.astype(jnp.bfloat16)
 
-    for d in (2, 1, 3):
-        terms[d - 1] = term(d)
-        term_copy(d).start()
-    summed = term(0).astype(jnp.float32)
-    for d in (1, 3, 2):
-        term_copy(d).wait()
-        summed += landed[d - 1].astype(jnp.float32)
-    out[...] = summed.astype(jnp.bfloat16)
+    own_terms = []
+    for t in range(2):
+        lax.fori_loop(2 * t, 2 * t + 2, attend, 0)
+        if t == 0:
+            run(steps_out, 9)
+        shares = mixed_rows(t)
+        for d in (2, 1, 3):
+            terms[d - 1, HALF * t : HALF * (t + 1), :] = term(shares, d)
+            term_copy(t, d).start()
+        own_terms.append(term(shares, 0).astype(jnp.float32))
+    for t in range(2):
+        summed = own_terms[t]
+        for d in (1, 3, 2):
+            term_copy(t, d).wait()
+            summed += landed[d - 1, HALF * t : HALF * (t + 1), :].astype(jnp.float32)
+        out[HALF * t : HALF * (t + 1), :] = summed.astype(jnp.bfloat16)
 
 
 def per_device(
@@ -470,8 +488,10 @@
             pltpu.VMEM((N_TP, TOK, 512), bf16),
             pltpu.VMEM((2048, 128), bf16),
             pltpu.VMEM((2048, 128), bf16),
-            pltpu.VMEM((2, NY, NZ, NX, 32, 384), bf16),
-            pltpu.VMEM((2, NY, NZ, NX, 32, 256), bf16),
+            pltpu.VMEM((NY, NZ, NX, 32, 384), bf16),
+            pltpu.VMEM((NY, NZ, NX, 32, 384), bf16),
+            pltpu.VMEM((NY, NZ, NX, 32, 128), bf16),
+            pltpu.VMEM((NY, NZ, NX, 32, 384), bf16),
             pltpu.VMEM((N_TP, TOK, 512), bf16),
             pltpu.VMEM((ROW_BLOCKS, 2 * TOK, 128), bf16),
             pltpu.VMEM((ROW_BLOCKS, 2 * TOK, 128), f32),
@@ -483,8 +503,8 @@
             pltpu.SemaphoreType.DMA((n_keys,)),
             pltpu.SemaphoreType.DMA((n_keys,)),
             pltpu.SemaphoreType.DMA((n_keys,)),
-            pltpu.SemaphoreType.DMA((7,)),
-            pltpu.SemaphoreType.DMA((7,)),
+            pltpu.SemaphoreType.DMA((10,)),
+            pltpu.SemaphoreType.DMA((10,)),
             pltpu.SemaphoreType.DMA((2,)),
         ],
         compiler_params=pltpu.CompilerParams(

time: 77.2 us -> 71.4 us (0.925)
  Pallas kernels: 71.5 us -> 66.2 us
    pallas_call x1, Pallas kernels: 71.5 us -> 66.2 us  [per_device(): pl.pallas_call(kernel, out_shape=(jax.ShapeDtypeStruct((TOK, 512), bf16),...]
where the time goes in v3:
time: 71.4 us; the launch traced here: 71.1 us
  Pallas kernels  66.2 us (93%)
  local copies, waits for them, and re-layouts  4.25 us (6%)
    pallas_call x1, Pallas kernels, per_device(): pl.pallas_call(kernel, out_shape=(jax.ShapeDtypeStruct((TOK, 512), bf16),...  66.2 us
    unnamed x9, local copies, waits for them, and re-layouts  3.64 us

profile of v3, /device:TPU:1, one launch (start us, length us, event | category | flops | bytes accessed | tf_op | source)
XLA Modules:
  0.0 71.1 jit_solution(4185438170707172858)
XLA Ops:
  0.6 0.0 copy-start.2
  0.6 0.7 copy-done.2
  1.3 0.6 reshape.9.gain
  1.9 66.2 %shard_map.121 = (bf16[128,512]{1,0:T(8,128)(2,1)}, bf16[128,128]{1,0:T(8,128)(2,1)}, bf16[128,128]{1,0:T(8,128)(2,1)}) custom-call(s32[128]{0:T(128)} %lengths.1, bf16[128,512]{1,0:T(8,128)(2,1)} %bitcast.10, bf16[1,2048]{1,0:T(2,128)(2,1)} %reshape.9.gain, f32[1,128]{1,0:T(1,128)} %constant.2.clone.inverse, bf16[16,512]{1,0:T(8,128)(2,1)} %w_query.1, ...), custom_call_target="tpu_custom_call" | custom-call | tf_op jit(solution)/shard_map/pallas_call | solution.py:478
  68.2 0.0 copy-start.1
  68.2 1.6 %copy.16 = bf16[1,128,512]{2,1,0:T(8,128)(2,1)} copy(bf16[1,128,512]{2,1,0:T(8,128)(2,1)} %bitcast.9) | data formatting | bytes 262144
  69.8 0.0 copy-done.1
  69.8 0.0 copy-start
  69.8 0.6 copy.17
  70.4 0.2 copy-done
  70.5 0.6 copy.18
Async XLA Ops:
  0.6 0.7 copy-start.2
  68.2 1.6 %copy-start.1 = (bf16[128,128]{1,0:T(8,128)(2,1)S(1)}, bf16[128,128]{1,0:T(8,128)(2,1)}, u32[]{:S(2)}) copy-start(bf16[128,128]{1,0:T(8,128)(2,1)} %get-tuple-element.7) | copy-start | bytes 98308
  69.8 0.8 %copy-start = (bf16[128,128]{1,0:T(8,128)(2,1)S(1)}, bf16[128,128]{1,0:T(8,128)(2,1)}, u32[]{:S(2)}) copy-start(bf16[128,128]{1,0:T(8,128)(2,1)} %get-tuple-element.8) | copy-start | bytes 98308

commit v4 on v3

--- a/solution.py
+++ b/solution.py
@@ -35,6 +35,8 @@
 RING = {a: ring_keys(a, SIZE[a]) for a in SIZE}
 DIRECT = {"x": [("direct", "x", k, u) for u in (0, 1) for k in (2, 1, 3)]}
 STAGES = {0: ("x", "z"), 1: ("z", "x")}
+HOPS = {0: {"z": {1: 1, 2: 2, 3: 1, 4: 2}}, 1: {"z": {1: 1, 2: 2, 3: 1, 4: 2}, "x": {1: 1, 2: 1}}}
+ORDER = {"z": (2, 1, 3, 4), "x": (1, 2)}
 FIRST = {"x": DIRECT["x"], "z": RING["z"]}
 PASS = {c: [("own", 0), ("own", 1)] + RING[STAGES[c][1]] for c in (0, 1)}
 KEYS = (
@@ -115,8 +117,9 @@
         else:
             axis, d, s, u = key
             pick = self.first_block if axis == STAGES[c][0] else self.second_block
-            src = dst = pick(c, u, axis, p.along(axis, -d * (s - 1)))
-            dev = p.device(**{axis: p.along(axis, d)})
+            hops = HOPS[c][axis][s]
+            src = dst = pick(c, u, axis, p.along(axis, -d * (s - hops)))
+            dev = p.device(**{axis: p.along(axis, d * hops)})
         return pltpu.make_async_remote_copy(
             src_ref=src,
             dst_ref=dst,
@@ -142,10 +145,19 @@
             for k in n_parts:
                 self.start(c, ("local", k))
 
+        def relay(axis, held, u, ways=(1, -1)):
+            for s in ORDER[axis]:
+                for d in ways:
+                    if s - HOPS[c][axis][s] == held and (axis, d, s, u) in KEY_INDEX:
+                        self.start(c, (axis, d, s, u))
+
         def start_first(u):
-            for key in FIRST[first]:
-                if key[3] == u and (key[0] == "direct" or key[2] == 1):
-                    self.start(c, key)
+            if first == "z":
+                relay(first, 0, u)
+            else:
+                for key in DIRECT[first]:
+                    if key[3] == u:
+                        self.start(c, key)
 
         def own():
             for k in n_parts:
@@ -159,8 +171,7 @@
             start_first(1)
 
         def enter_second(u):
-            for d in (1, -1):
-                self.start(c, (second, d, 1, u))
+            relay(second, 0, u)
             self.start(c, ("pass", c, ("own", u)))
 
         def after_direct():
@@ -175,17 +186,15 @@
                 _, d, s, u = key
                 if s == step:
                     self.land(c, key)
-                    if s == SIZE[first] // 2:
+                    relay(first, s, u, (d,))
+                    if s == ORDER[first][-1]:
                         enter_second(u)
-                    elif (first, d, s + 1, u) in KEY_INDEX:
-                        self.start(c, (first, d, s + 1, u))
 
         def ring_step(keys):
             for key in keys:
                 _, d, s, u = key
                 self.land(c, key)
-                if (second, d, s + 1, u) in KEY_INDEX:
-                    self.start(c, (second, d, s + 1, u))
+                relay(second, s, u, (d,))
                 self.start(c, ("pass", c, key))
 
         def finish():
@@ -198,8 +207,8 @@
         if first == "x":
             middle = [after_direct]
         else:
-            middle = [functools.partial(first_step, i) for i in range(1, SIZE[first] // 2 + 1)]
-        for i in range(1, SIZE[second] // 2 + 1):
+            middle = [functools.partial(first_step, i) for i in ORDER[first]]
+        for i in ORDER[second]:
             middle.append(functools.partial(ring_step, [k for k in RING[second] if k[2] == i]))
         middle += [lambda: None] * (6 - len(middle))
         return [begin, own, other] + middle + [finish]
@@ -260,7 +269,7 @@
         partners += [
             place.device(**{axis: place.along(axis, k)})
             for k in range(1, SIZE[axis])
-            if axis == "x" or k in (1, SIZE[axis] - 1)
+            if axis == "x" or min(k, SIZE[axis] - k) <= 2
         ]
     others = [lax.rem(place.tp + d, N_TP) for d in range(N_TP)]
     partners += [place.device(tp=others[d]) for d in range(1, N_TP)]
@@ -281,7 +290,7 @@
         [(w_query.at[:, pl.ds(256 * half, 256)], 0), ((w_key, w_value)[half], 256)]
         for half in (0, 1)
     ]
-    parts_out = [[(w_out.at[:, pl.ds(0, 128)], 0)], [(w_out.at[:, pl.ds(128, 384)], 0)]]
+    parts_out = [[(w_out.at[:, pl.ds(256 * half, 256)], 0)] for half in (0, 1)]
     buf_in, buf_out = (buf_in_0, buf_in_1), (buf_out_0, buf_out_1)
     gather_in = Gather(place, parts_in, buf_in, send_in, recv_in)
     gather_out = Gather(place, parts_out, buf_out, send_out, recv_out)
@@ -423,7 +432,7 @@
                 else:
                     tile = jnp.where(low, pltpu.roll(even, 64, 1), odd)
                 tiles.append(tile.astype(jnp.bfloat16))
-        return tiles[0], jnp.concatenate(tiles[1:], axis=1)
+        return jnp.concatenate(tiles[:2], axis=1), jnp.concatenate(tiles[2:], axis=1)
 
     def term_copy(t, d):
         return pltpu.make_async_remote_copy(
@@ -490,8 +499,8 @@
             pltpu.VMEM((2048, 128), bf16),
             pltpu.VMEM((NY, NZ, NX, 32, 384), bf16),
             pltpu.VMEM((NY, NZ, NX, 32, 384), bf16),
-            pltpu.VMEM((NY, NZ, NX, 32, 128), bf16),
-            pltpu.VMEM((NY, NZ, NX, 32, 384), bf16),
+            pltpu.VMEM((NY, NZ, NX, 32, 256), bf16),
+            pltpu.VMEM((NY, NZ, NX, 32, 256), bf16),
             pltpu.VMEM((N_TP, TOK, 512), bf16),
             pltpu.VMEM((ROW_BLOCKS, 2 * TOK, 128), bf16),
             pltpu.VMEM((ROW_BLOCKS, 2 * TOK, 128), f32),

time: 71.4 us -> 69.4 us (0.972)
  Pallas kernels: 66.2 us -> 64.2 us
    pallas_call x1, Pallas kernels: 66.2 us -> 64.2 us  [per_device(): pl.pallas_call(kernel, out_shape=(jax.ShapeDtypeStruct((TOK, 512), bf16),...]
where the time goes in v4:
time: 69.4 us; the launch traced here: 69.1 us
  Pallas kernels  64.2 us (93%)
  local copies, waits for them, and re-layouts  4.25 us (6%)
    pallas_call x1, Pallas kernels, per_device(): pl.pallas_call(kernel, out_shape=(jax.ShapeDtypeStruct((TOK, 512), bf16),...  64.2 us
    unnamed x9, local copies, waits for them, and re-layouts  3.64 us

profile of v4, /device:TPU:1, one launch (start us, length us, event | category | flops | bytes accessed | tf_op | source)
XLA Modules:
  0.0 69.1 jit_solution(1365157106465376624)
XLA Ops:
  0.6 0.0 copy-start.2
  0.6 0.7 copy-done.2
  1.3 0.6 reshape.9.gain
  1.9 64.2 %shard_map.121 = (bf16[128,512]{1,0:T(8,128)(2,1)}, bf16[128,128]{1,0:T(8,128)(2,1)}, bf16[128,128]{1,0:T(8,128)(2,1)}) custom-call(s32[128]{0:T(128)} %lengths.1, bf16[128,512]{1,0:T(8,128)(2,1)} %bitcast.10, bf16[1,2048]{1,0:T(2,128)(2,1)} %reshape.9.gain, f32[1,128]{1,0:T(1,128)} %constant.2.clone.inverse, bf16[16,512]{1,0:T(8,128)(2,1)} %w_query.1, ...), custom_call_target="tpu_custom_call" | custom-call | tf_op jit(solution)/shard_map/pallas_call | solution.py:487
  66.1 0.0 copy-start.1
  66.1 1.6 %copy.16 = bf16[1,128,512]{2,1,0:T(8,128)(2,1)} copy(bf16[1,128,512]{2,1,0:T(8,128)(2,1)} %bitcast.9) | data formatting | bytes 262144
  67.7 0.0 copy-done.1
  67.7 0.0 copy-start
  67.7 0.6 copy.17
  68.3 0.2 copy-done
  68.5 0.6 copy.18
Async XLA Ops:
  0.6 0.7 copy-start.2
  66.1 1.6 %copy-start.1 = (bf16[128,128]{1,0:T(8,128)(2,1)S(1)}, bf16[128,128]{1,0:T(8,128)(2,1)}, u32[]{:S(2)}) copy-start(bf16[128,128]{1,0:T(8,128)(2,1)} %get-tuple-element.7) | copy-start | bytes 98308
  67.7 0.8 %copy-start = (bf16[128,128]{1,0:T(8,128)(2,1)S(1)}, bf16[128,128]{1,0:T(8,128)(2,1)}, u32[]{:S(2)}) copy-start(bf16[128,128]{1,0:T(8,128)(2,1)} %get-tuple-element.8) | copy-start | bytes 98308

commit v5 on v4

--- a/solution.py
+++ b/solution.py
@@ -337,6 +337,7 @@
     own_rows.wait()
     for d in (1, 2, 3):
         hidden_copy(d).wait()
+    gain_row = gain[...].astype(jnp.float32).reshape(1, 512 * N_TP)
     squares = 0.0
     for j in range(N_TP):
         part = rows[j].astype(jnp.float32)
@@ -344,7 +345,7 @@
     scale = lax.rsqrt(squares * (1.0 / (512 * N_TP)) + norm_eps)
     for j in range(N_TP):
         part = rows[j].astype(jnp.float32)
-        normed[j] = (part * scale * gain[:, 512 * j : 512 * (j + 1)].astype(jnp.float32)).astype(
+        normed[j] = (part * scale * gain_row[:, 512 * j : 512 * (j + 1)]).astype(
             jnp.bfloat16
         )
 
@@ -522,7 +523,7 @@
     )(
         cache_lengths,
         hidden[0],
-        norm_gain.reshape(1, -1),
+        norm_gain,
         jnp.asarray(inverse),
         w_query,
         w_key,

time: 69.4 us -> 68 us (0.980)
  local copies, waits for them, and re-layouts: 4.25 us -> 2.96 us
    unnamed x9 -> x7, local copies, waits for them, and re-layouts: 3.64 us -> 2.96 us
where the time goes in v5:
time: 68 us; the launch traced here: 67.8 us
  Pallas kernels  64.2 us (94%)
  local copies, waits for them, and re-layouts  2.96 us (4%)
    pallas_call x1, Pallas kernels, per_device(): pl.pallas_call(kernel, out_shape=(jax.ShapeDtypeStruct((TOK, 512), bf16),...  64.2 us
    unnamed x7, local copies, waits for them, and re-layouts  2.96 us

profile of v5, /device:TPU:1, one launch (start us, length us, event | category | flops | bytes accessed | tf_op | source)
XLA Modules:
  0.0 67.8 jit_solution(1827257561900008119)
XLA Ops:
  0.6 64.2 %shard_map.121 = (bf16[128,512]{1,0:T(8,128)(2,1)}, bf16[128,128]{1,0:T(8,128)(2,1)}, bf16[128,128]{1,0:T(8,128)(2,1)}) custom-call(s32[128]{0:T(128)} %lengths.1, bf16[128,512]{1,0:T(8,128)(2,1)} %bitcast.10, bf16[2048]{0:T(1024)(128)(2,1)} %gain.1, f32[1,128]{1,0:T(1,128)} %constant.2.clone.inverse, bf16[16,512]{1,0:T(8,128)(2,1)} %w_query.1, ...), custom_call_target="tpu_custom_call" | custom-call | tf_op jit(solution)/shard_map/pallas_call | solution.py:488
  64.8 0.0 copy-start.1
  64.8 1.6 %copy.16 = bf16[1,128,512]{2,1,0:T(8,128)(2,1)} copy(bf16[1,128,512]{2,1,0:T(8,128)(2,1)} %bitcast.9) | data formatting | bytes 262144
  66.4 0.0 copy-done.1
  66.4 0.0 copy-start
  66.4 0.6 copy.17
  67.0 0.2 copy-done
  67.2 0.6 copy.18
Async XLA Ops:
  64.8 1.6 %copy-start.1 = (bf16[128,128]{1,0:T(8,128)(2,1)S(1)}, bf16[128,128]{1,0:T(8,128)(2,1)}, u32[]{:S(2)}) copy-start(bf16[128,128]{1,0:T(8,128)(2,1)} %get-tuple-element.7) | copy-start | bytes 98308
  66.4 0.8 %copy-start = (bf16[128,128]{1,0:T(8,128)(2,1)S(1)}, bf16[128,128]{1,0:T(8,128)(2,1)}, u32[]{:S(2)}) copy-start(bf16[128,128]{1,0:T(8,128)(2,1)} %get-tuple-element.8) | copy-start | bytes 98308
